TPU v7x, 512 devices: a whole 4x4x16 slice. The times are simulated.
512 devices in a mesh: takers: 64 (over z, x), nodes: 8 (over y, core).
Axes of the slice: x: 4, y: 4, z: 16, core: 2. Of those that a mesh axis runs over, the one named last changes fastest.
Arguments:
- slopes: bfloat16 [3, 65536], P(None, 'takers'), may hold values from 0.29882812 to 1.5
- intercepts: bfloat16 [65536], P('takers'), may hold values from -3 to 3
- guessing: bfloat16 [65536], P('takers'), may hold values from 0.049804688 to 0.29882812
- responses: int32 [256, 12, 128, 128], P('takers'), may hold values from 0 to 2, as said below
- tile_items: int32 [256, 12], P('takers'), may hold values from 0 to 511, as said below
- tile_count: int32 [256], P('takers'), may hold values from 4 to 12, as said below
Outputs:
- new_params: float32 [4, 65536], P(None, 'takers')
- marginal: float32 [32768], P('takers')
- posterior_mean: float32 [3, 32768], P(None, 'takers')
Inputs may be any that keep to these rules, and one draw needn't show every extreme that they name: `tile_items`: within a row block the used slots name distinct item blocks; some row block uses all 12 slots. `tile_count`: some row block uses all 12 slots; slots at or beyond the count are ignored. `responses`: 0 means not answered, 1 a wrong answer, 2 a right answer; most entries are 0.
All inputs are finite; a program needn't handle non-finite values.
Results may differ from a plain program's by a relative error of at most 0.0041.
Values may be sent and summed in bfloat16 or wider, within the bound.
No kernel may reach another device: no remote copies, remote signals or barrier semaphores. Data moves between devices by JAX's collectives and lax.ppermute only.
A program may use at most 64 MiB of HBM per device.

v0:
```python
import jax
import jax.numpy as jnp
from jax import lax
from jax.sharding import PartitionSpec as P

NODES_1D = 16


def node_grid(first_node, how_many, grid_side):
    node_index = first_node + jnp.arange(how_many, dtype=jnp.int32)
    lattice = jnp.stack(
        [
            node_index // (grid_side * grid_side),
            node_index // grid_side % grid_side,
            node_index % grid_side,
        ]
    ).astype(jnp.float32)
    return -3.0 + 6.0 * lattice / (grid_side - 1)


def log_prior(node_points, grid_side):
    whole = node_grid(0, grid_side**3, grid_side)
    log_total = jnp.log(jnp.sum(jnp.exp(-0.5 * jnp.sum(whole * whole, axis=0))))
    return -0.5 * jnp.sum(node_points * node_points, axis=0) - log_total


def tile_logits(slope_blk, icpt_blk, node_points):
    return (
        slope_blk[:, 0, :, None] * node_points[0]
        + slope_blk[:, 1, :, None] * node_points[1]
        + slope_blk[:, 2, :, None] * node_points[2]
        + icpt_blk[:, :, None]
    )


def apply_update(summed, own_slopes, own_icpt):
    current = jnp.concatenate(
        [own_slopes.astype(jnp.float32), own_icpt.astype(jnp.float32)[None]], axis=0
    )
    return current + summed[:4] / (summed[4:] + 1.0)


def indicators(answers):
    right_b = (answers == 2).astype(jnp.bfloat16)
    answered_b = (answers > 0).astype(jnp.bfloat16)
    wrong_b = (answers == 1).astype(jnp.bfloat16)
    return (right_b, wrong_b, answered_b)


def local(slopes, intercepts, guessing, responses, tile_items, tile_count):
    grid_side = NODES_1D
    tile_size = responses.shape[-1]
    slot_count = responses.shape[1]
    nodes_here = grid_side**3 // lax.axis_size("nodes")
    node_points = node_grid(lax.axis_index("nodes") * nodes_here, nodes_here, grid_side)
    prior_here = log_prior(node_points, grid_side)
    features = jnp.concatenate([node_points, jnp.ones((1, nodes_here), jnp.float32)], axis=0)
    all_slopes, all_icpt, all_guess = (
        lax.all_gather(slopes, "takers", axis=1, tiled=True),
        lax.all_gather(intercepts, "takers", axis=0, tiled=True),
        lax.all_gather(guessing, "takers", axis=0, tiled=True),
    )
    blocks = all_icpt.shape[0] // tile_size
    slope_tab = all_slopes.astype(jnp.float32).reshape(3, blocks, tile_size)
    icpt_tab = all_icpt.astype(jnp.float32).reshape(blocks, tile_size)
    guess_tab = all_guess.astype(jnp.float32).reshape(blocks, tile_size)

    def tables(block_ids, filled):
        live_mask = (jnp.arange(slot_count, dtype=jnp.int32) < filled).astype(jnp.float32)[
            :, None, None
        ]
        slope_blk = jnp.transpose(slope_tab[:, block_ids], (1, 0, 2))
        logits = tile_logits(slope_blk, icpt_tab[block_ids], node_points)
        return (logits, guess_tab[block_ids][:, :, None], live_mask)

    def loglik_block(inputs):
        answers, block_ids, filled = inputs
        logits, guess_rate, live_mask = tables(block_ids, filled)
        correct = guess_rate + (1.0 - guess_rate) * jax.nn.sigmoid(logits)
        log_miss = jnp.log(1.0 - guess_rate) + jax.nn.log_sigmoid(-logits)
        log_right = (jnp.log(correct) * live_mask).astype(jnp.bfloat16)
        log_wrong = (log_miss * live_mask).astype(jnp.bfloat16)
        right_b, wrong_b, answered_b = indicators(answers)
        stacked_ind = jnp.stack([right_b, wrong_b])
        stacked_tab = jnp.stack([log_right, log_wrong])
        matched = lax.dot_general(
            stacked_ind,
            stacked_tab,
            (((0, 1, 3), (0, 1, 2)), ((), ())),
            preferred_element_type=jnp.float32,
        )
        return matched + prior_here

    loglik = lax.map(loglik_block, (responses, tile_items, tile_count)).reshape(-1, nodes_here)
    row_max = jnp.max(loglik, axis=1)
    global_max = lax.pmax(row_max, "nodes")
    weights = jnp.exp(loglik - global_max[:, None])
    moment_here = jnp.einsum("cq,tq->ct", node_points, weights, precision=lax.Precision.HIGHEST)
    row_mass, moment = lax.psum((jnp.sum(weights, axis=1), moment_here), "nodes")
    log_norm = global_max + jnp.log(row_mass)
    posterior_mean = moment / row_mass
    posterior = (
        jnp.exp(loglik - log_norm[:, None]).astype(jnp.bfloat16).reshape(-1, tile_size, nodes_here)
    )

    def stats_block(inputs):
        answers, block_ids, filled, post_blk = inputs
        logits, guess_rate, live_mask = tables(block_ids, filled)
        sig_pos = jax.nn.sigmoid(logits)
        sig_neg = jax.nn.sigmoid(-logits)
        correct = guess_rate + (1.0 - guess_rate) * sig_pos
        right_b, wrong_b, answered_b = indicators(answers)
        stacked_ind = jnp.stack([right_b, answered_b])
        both_mass = lax.dot_general(
            stacked_ind, post_blk, (((2,), (0,)), ((), ())), preferred_element_type=jnp.float32
        )
        correct_mass = both_mass[0]
        node_mass = both_mass[1]
        gradient = (correct_mass - node_mass * correct) * (sig_pos / correct) * live_mask
        fisher = node_mass * (1.0 - guess_rate) * sig_pos * sig_pos * sig_neg / correct * live_mask
        grad_terms = jnp.einsum("kiq,cq->kci", gradient, features, precision=lax.Precision.HIGHEST)
        fisher_terms = jnp.einsum(
            "kiq,cq->kci", fisher, features * features, precision=lax.Precision.HIGHEST
        )
        return jnp.concatenate([grad_terms, fisher_terms], axis=1)

    tile_stats = lax.map(stats_block, (responses, tile_items, tile_count, posterior))
    flat_stats = jnp.transpose(tile_stats, (2, 0, 1, 3)).reshape(8, -1, tile_size)
    item_totals = (
        jnp.zeros((8, blocks, tile_size), jnp.float32).at[:, tile_items.reshape(-1)].add(flat_stats)
    )
    item_totals = item_totals.reshape(8, blocks * tile_size)
    summed = lax.psum_scatter(item_totals, "takers", scatter_dimension=1, tiled=True)
    summed = lax.psum(summed, "nodes")
    new_params = apply_update(summed, slopes, intercepts)
    return (new_params, log_norm, posterior_mean)


def solution(mesh):
    in_specs = (
        P(None, "takers"),
        P("takers"),
        P("takers"),
        P("takers", None, None, None),
        P("takers", None),
        P("takers"),
    )
    out_specs = (P(None, "takers"), P("takers"), P(None, "takers"))
    return jax.shard_map(local, mesh=mesh, in_specs=in_specs, out_specs=out_specs, check_vma=False)
```

profile of v0, /device:TPU:2, one launch (start us, length us, event | category | flops | bytes accessed | tf_op | source)
XLA Modules:
  0.0 1167.5 jit_solution(3456560826222330985)
XLA Ops:
  10.2 105.5 %all_gather.9 = bf16[65536]{0:T(1024)(128)(2,1)S(1)} all-gather(bf16[1024]{0:T(1024)(128)(2,1)} %param.12), channel_id=1, replica_groups=mesh['takers'=64,'nodes'=8] {'takers'}, dimensions={0}, use_global_device_ids=true | all-gather | bytes 133120 | tf_op jit(solution)/shard_map/all_gather | solution.py:61
  115.7 97.4 %all_gather.11 = bf16[65536]{0:T(1024)(128)(2,1)S(1)} all-gather(bf16[1024]{0:T(1024)(128)(2,1)} %param.11), channel_id=1, replica_groups=mesh['takers'=64,'nodes'=8] {'takers'}, dimensions={0}, use_global_device_ids=true | all-gather | bytes 133120 | tf_op jit(solution)/shard_map/all_gather | solution.py:60
  213.1 98.1 %all_gather.10 = bf16[3,65536]{1,0:T(4,128)(2,1)S(1)} all-gather(bf16[3,1024]{1,0:T(4,128)(2,1)} %param.10), channel_id=1, replica_groups=mesh['takers'=64,'nodes'=8] {'takers'}, dimensions={1}, use_global_device_ids=true | all-gather | bytes 399360 | tf_op jit(solution)/shard_map/all_gather | solution.py:59
  311.5 36.9 %while.21 = (s32[]{:T(128)}, f32[4,128,512]{2,1,0:T(8,128)S(1)}, s32[4,12,128,128]{3,2,1,0:T(8,128)}, s32[4,12]{1,0:T(4,128)S(1)}, f32[512,128]{1,0:T(8,128)S(1)...) while((s32[]{:T(128)}, f32[4,128,512]{2,1,0:T(8,128)S(1)}, ...), condition=%wide.region_4.5_spmd, body=%wide.region_3.4_spmd.sunk | while | flops 423168576 | bytes 8348177 | solution.py:94
  314.5 1.4 dynamic-slice_compare_fusion.3
  315.9 4.2 multiply_convert_fusion.2
  323.8 1.4 dynamic-slice_compare_fusion.3
  325.1 4.2 multiply_convert_fusion.2
  333.0 1.4 dynamic-slice_compare_fusion.3
  334.4 4.2 multiply_convert_fusion.2
  342.2 1.4 dynamic-slice_compare_fusion.3
  343.6 4.2 multiply_convert_fusion.2
  348.6 12.4 %pmax.7 = f32[512]{0:T(512)S(1)} all-reduce(f32[512]{0:T(512)S(1)} %bitcast.192), channel_id=1, replica_groups=mesh['takers'=64,'nodes'=8] {'nodes'}, use_global_device_ids=true, to_apply=%region_6.7 | all-reduce | flops 512 | bytes 4096 | tf_op jit(solution)/shard_map/pmax | solution.py:96
  361.3 12.7 %psum.21 = f32[512]{0:T(512)S(1)} all-reduce(f32[512]{0:T(512)S(1)} %bitcast.193), channel_id=1, replica_groups=mesh['takers'=64,'nodes'=8] {'nodes'}, use_global_device_ids=true, to_apply=%region_8.9 | all-reduce | flops 512 | bytes 4096 | tf_op jit(solution)/shard_map/psum | solution.py:99
  375.0 69.3 %while.22 = (s32[]{:T(128)}, f32[4,12,8,128]{3,2,1,0:T(8,128)S(1)}, s32[4,12,128,128]{3,2,1,0:T(8,128)}, bf16[4,128,512]{2,1,0:T(8,128)(2,1)}, s32[4,12]{1,0:T(4...) while((s32[]{:T(128)}, f32[4,12,8,128]{3,2,1,0:T(8,128)S(1)}, ...), condition=%wide.region_10.11_spmd, body=%wide.region_9.10_spmd.sunk | while | flops 507263552 | bytes 27296860 | solution.py:127
  378.2 1.2 constant_dynamic-slice_fusion.4
  379.9 1.9 fusion.147
  381.8 5.1 fusion.152
  386.8 5.4 fusion.151
  397.2 1.9 fusion.147
  399.1 5.1 fusion.152
  404.2 5.4 fusion.151
  414.5 1.9 fusion.147
  416.4 5.1 fusion.152
  421.5 5.4 fusion.151
  431.9 1.9 fusion.147
  433.7 5.1 fusion.152
  438.8 5.4 fusion.151
  444.5 2.2 scatter_fusion
  446.7 1.3 copy-done
  449.3 685.7 %reduce-scatter.2.cloned.1.call-done = f32[8,1024]{1,0:T(8,128)} async-done(((f32[8,65536]{1,0:T(8,128)}), f32[8,1024]{1,0:T(8,128)}) %reduce-scatter.2.cloned.1.call-update) | async-done | bytes 32784 | tf_op jit(solution)/shard_map/reduce_scatter | solution.py:133
  1135.0 24.5 %all-reduce.1 = (f32[8,1024]{1,0:T(8,128)S(1)}, f32[3,512]{1,0:T(4,128)S(1)}) all-reduce(f32[8,1024]{1,0:T(8,128)} %reduce-scatter.2.cloned.1.call-done, f32[3,512]{1,0:T(4,128)S(1)} %fusion.109), channel_id=1, replica_groups=mesh['takers'=64,'nodes'=8] {'nodes'}, use_global_device_ids=true, to_apply=%region_13.14 | all-reduce | flops 9728 | bytes 77824 | tf_op jit(solution)/shard_map/psum | solution.py:134
  (184 shorter events, 38.8 us)
Async XLA Ops:
  7.2 304.3 %copy-start.12 = (s32[4,12]{1,0:T(4,128)S(1)}, s32[4,12]{1,0:T(4,128)}, u32[]{:S(2)}) copy-start(s32[4,12]{1,0:T(4,128)} %param.14) | copy-start | bytes 580
  7.2 304.3 %copy-start.14 = (s32[4]{0:T(128)S(1)}, s32[4]{0:T(128)}, u32[]{:S(2)}) copy-start(s32[4]{0:T(128)} %param.15) | copy-start | bytes 52
  7.2 1127.8 %reduce-scatter.2.cloned.1.call-start = ((), (), s32[]{:S(2)}) async-start(), calls=%async_computation.1 | async-start | bytes 2129920 | tf_op jit(solution)/shard_map/reduce_scatter | solution.py:133
  7.3 304.2 %copy-start.4 = (s32[1,512]{1,0:T(1,128)}, s32[1,512]{1,0:T(1,128)S(1)}, u32[]{:S(2)}) copy-start(s32[1,512]{1,0:T(1,128)S(1)} %and_select_fusion.7) | copy-start | bytes 6148
  7.3 1.4 copy-start.8
  7.3 304.1 %copy-start.6 = (s32[1,512]{1,0:T(1,128)}, s32[1,512]{1,0:T(1,128)S(1)}, u32[]{:S(2)}) copy-start(s32[1,512]{1,0:T(1,128)S(1)} %get-tuple-element.285) | copy-start | bytes 6148
  374.0 1.0 copy-start.11
  375.0 69.5 %copy-start.13 = (s32[48]{0:T(128)S(1)}, s32[48]{0:T(128)}, u32[]{:S(2)}) copy-start(s32[48]{0:T(128)} %fusion.108) | copy-start | bytes 580
  375.0 3.2 copy-start.1
  386.8 5.5 copy-start.2
  392.3 3.2 copy-start.1
  404.2 5.5 copy-start.2
  409.7 3.2 copy-start.1
  421.5 5.5 copy-start.2
  427.0 3.2 copy-start.1
  438.8 5.5 copy-start.2
  444.3 3.8 copy-start.10
  444.3 4.0 copy-start.5
  444.3 4.0 copy-start.7
  444.4 4.0 copy-start.9
  444.5 715.5 %copy-start.3 = (bf16[3,1024]{1,0:T(4,128)(2,1)S(1)}, bf16[3,1024]{1,0:T(4,128)(2,1)}, u32[]{:S(2)}) copy-start(bf16[3,1024]{1,0:T(4,128)(2,1)} %param.10) | copy-start | bytes 18436
  446.7 1.3 copy-start
Sparse Core Ops, SparseCore 0:
  448.2 686.7 reduce-scatter.1
where the time goes:
time: 1170 us
  waiting for transfers between devices  686 us (59%)
  blocking collectives  351 us (30%)
  matrix products  52.9 us (5%)
  other arithmetic  35.2 us (3%)
  local copies, waits for them, and re-layouts  27.2 us (2%)
  between operations  15 us (1%)
    reduce_scatter x1, waiting for transfers between devices, local(): lax.psum_scatter(item_totals, 'takers', scatter_dimension=1, tiled=True)  686 us
    all_gather x1, blocking collectives, local(): lax.all_gather(guessing, 'takers', axis=0, tiled=True)  106 us
    all_gather x1, blocking collectives, local(): lax.all_gather(slopes, 'takers', axis=1, tiled=True)  98.1 us
    all_gather x1, blocking collectives, local(): lax.all_gather(intercepts, 'takers', axis=0, tiled=True)  97.4 us
    psum x1, blocking collectives, local(): summed = lax.psum(summed, 'nodes')  24.5 us
  transfers between devices with their start and end apart: 1, of which 1 were waited for; matrix products, arithmetic and copies ran while one was open for 0% of the time, Pallas kernels for 0%

commit v1 on v0

--- a/solution.py
+++ b/solution.py
@@ -4,6 +4,9 @@
 from jax.sharding import PartitionSpec as P
 
 NODES_1D = 16
+derive_slices = lambda frame: jnp.concatenate(
+    lax.all_to_all(jnp.stack([frame] * lax.axis_size("takers"), axis=0), "takers", 0, 0), axis=0
+)
 
 
 def node_grid(first_node, how_many, grid_side):
@@ -58,7 +61,7 @@
     all_slopes, all_icpt, all_guess = (
         lax.all_gather(slopes, "takers", axis=1, tiled=True),
         lax.all_gather(intercepts, "takers", axis=0, tiled=True),
-        lax.all_gather(guessing, "takers", axis=0, tiled=True),
+        derive_slices(guessing),
     )
     blocks = all_icpt.shape[0] // tile_size
     slope_tab = all_slopes.astype(jnp.float32).reshape(3, blocks, tile_size)

time: 1170 us -> 1090 us (0.932)
  blocking collectives: 351 us -> 247 us
  starting transfers between devices: 0.04 us -> 18.7 us
    all_gather x1 -> x0, blocking collectives: 106 us -> none  [local(): lax.all_gather(guessing, 'takers', axis=0, tiled=True)]
    all_to_all x0 -> x1, starting transfers between devices: none -> 18.6 us  [lax.all_to_all(jnp.stack([frame] * lax.axis_size('takers'), axis=0), 'tak...]
  transfers between devices with their start and end apart: 1 -> 2, of which waited for: 1 -> 1; matrix products, arithmetic and copies ran while one was open for 0% -> 0% of each run, Pallas kernels for 0% -> 0%
where the time goes in v1:
time: 1090 us
  waiting for transfers between devices  688 us (63%)
  blocking collectives  247 us (23%)
  matrix products  52.9 us (5%)
  other arithmetic  36.9 us (3%)
  local copies, waits for them, and re-layouts  29.7 us (3%)
  starting transfers between devices  18.7 us (2%)
  between operations  15 us (1%)
    reduce_scatter x1, waiting for transfers between devices, local(): lax.psum_scatter(item_totals, 'takers', scatter_dimension=1, tiled=True)  688 us
    all_gather x1, blocking collectives, local(): lax.all_gather(slopes, 'takers', axis=1, tiled=True)  99.8 us
    all_gather x1, blocking collectives, local(): lax.all_gather(intercepts, 'takers', axis=0, tiled=True)  97.5 us
    psum x1, blocking collectives, local(): summed = lax.psum(summed, 'nodes')  24.5 us
  transfers between devices with their start and end apart: 2, of which 1 were waited for; matrix products, arithmetic and copies ran while one was open for 0% of the time, Pallas kernels for 0%

profile of v1, /device:TPU:2, one launch (start us, length us, event | category | flops | bytes accessed | tf_op | source)
XLA Modules:
  0.0 1089.1 jit_solution(72841714430214098)
XLA Ops:
  8.5 1.4 reduce.2
  10.6 18.6 %all-to-all-start = ((bf16[64,2,512]{2,1,0:T(2,128)(2,1)}), bf16[64,2,512]{2,1,0:T(2,128)(2,1)S(1)}, u32[]{:S(2)}, u32[]{:S(2)}) async-start(bf16[64,2,512]{2,1,0:T(2,128)(2,1)} %reshape.582), calls=%async_computation | async-start | bytes 262144 | tf_op jit(solution)/shard_map/all_to_all | solution.py:8
  32.4 99.8 %all_gather.6 = bf16[3,65536]{1,0:T(4,128)(2,1)S(1)} all-gather(bf16[3,1024]{1,0:T(4,128)(2,1)} %param.10), channel_id=1, replica_groups=mesh['takers'=64,'nodes'=8] {'takers'}, dimensions={1}, use_global_device_ids=true | all-gather | bytes 399360 | tf_op jit(solution)/shard_map/all_gather | solution.py:62
  132.2 97.5 %all_gather.7 = bf16[65536]{0:T(1024)(128)(2,1)S(1)} all-gather(bf16[1024]{0:T(1024)(128)(2,1)} %param.11), channel_id=1, replica_groups=mesh['takers'=64,'nodes'=8] {'takers'}, dimensions={0}, use_global_device_ids=true | all-gather | bytes 133120 | tf_op jit(solution)/shard_map/all_gather | solution.py:63
  230.2 37.1 %while.21 = (s32[]{:T(128)}, f32[4,128,512]{2,1,0:T(8,128)S(1)}, s32[4,12,128,128]{3,2,1,0:T(8,128)}, s32[4,12]{1,0:T(4,128)S(1)}, f32[512,128]{1,0:T(8,128)S(1)...) while((s32[]{:T(128)}, f32[4,128,512]{2,1,0:T(8,128)S(1)}, ...), condition=%wide.region_4.5_spmd, body=%wide.region_3.4_spmd.sunk | while | flops 423168576 | bytes 8348177 | solution.py:97
  233.4 1.4 dynamic-slice_compare_fusion.3
  234.7 4.2 multiply_convert_fusion.2
  242.6 1.4 dynamic-slice_compare_fusion.3
  244.0 4.2 multiply_convert_fusion.2
  251.9 1.4 dynamic-slice_compare_fusion.3
  253.3 4.2 multiply_convert_fusion.2
  261.2 1.4 dynamic-slice_compare_fusion.3
  262.5 4.2 multiply_convert_fusion.2
  267.5 12.4 %pmax.7 = f32[512]{0:T(512)S(1)} all-reduce(f32[512]{0:T(512)S(1)} %bitcast.191), channel_id=1, replica_groups=mesh['takers'=64,'nodes'=8] {'nodes'}, use_global_device_ids=true, to_apply=%region_6.7 | all-reduce | flops 512 | bytes 4096 | tf_op jit(solution)/shard_map/pmax | solution.py:99
  280.2 12.7 %psum.21 = f32[512]{0:T(512)S(1)} all-reduce(f32[512]{0:T(512)S(1)} %bitcast.192), channel_id=1, replica_groups=mesh['takers'=64,'nodes'=8] {'nodes'}, use_global_device_ids=true, to_apply=%region_8.9 | all-reduce | flops 512 | bytes 4096 | tf_op jit(solution)/shard_map/psum | solution.py:102
  293.9 69.5 %while.22 = (s32[]{:T(128)}, f32[4,12,8,128]{3,2,1,0:T(8,128)S(1)}, s32[4,12,128,128]{3,2,1,0:T(8,128)}, bf16[4,128,512]{2,1,0:T(8,128)(2,1)}, s32[4,12]{1,0:T(4...) while((s32[]{:T(128)}, f32[4,12,8,128]{3,2,1,0:T(8,128)S(1)}, ...), condition=%wide.region_10.11_spmd, body=%wide.region_9.10_spmd.sunk | while | flops 507263552 | bytes 27296860 | solution.py:130
  298.8 1.9 fusion.147
  300.7 5.1 fusion.152
  305.8 5.4 fusion.151
  316.2 1.9 fusion.147
  318.1 5.1 fusion.152
  323.2 5.4 fusion.151
  333.6 1.9 fusion.147
  335.5 5.1 fusion.152
  340.5 5.4 fusion.151
  351.0 1.9 fusion.147
  352.8 5.1 fusion.152
  357.9 5.4 fusion.151
  363.6 2.2 scatter_fusion
  365.8 1.3 copy-done
  368.4 688.2 %reduce-scatter.2.cloned.1.call-done = f32[8,1024]{1,0:T(8,128)} async-done(((f32[8,65536]{1,0:T(8,128)}), f32[8,1024]{1,0:T(8,128)}) %reduce-scatter.2.cloned.1.call-update) | async-done | bytes 32784 | tf_op jit(solution)/shard_map/reduce_scatter | solution.py:136
  1056.6 24.5 %all-reduce.1 = (f32[8,1024]{1,0:T(8,128)S(1)}, f32[3,512]{1,0:T(4,128)S(1)}) all-reduce(f32[8,1024]{1,0:T(8,128)} %reduce-scatter.2.cloned.1.call-done, f32[3,512]{1,0:T(4,128)S(1)} %fusion.109), channel_id=1, replica_groups=mesh['takers'=64,'nodes'=8] {'nodes'}, use_global_device_ids=true, to_apply=%region_13.14 | all-reduce | flops 9728 | bytes 77824 | tf_op jit(solution)/shard_map/psum | solution.py:137
  (190 shorter events, 42.9 us)
Async XLA Ops:
  7.2 223.0 %copy-start.12 = (s32[4,12]{1,0:T(4,128)S(1)}, s32[4,12]{1,0:T(4,128)}, u32[]{:S(2)}) copy-start(s32[4,12]{1,0:T(4,128)} %param.14) | copy-start | bytes 580
  7.2 223.0 %copy-start.14 = (s32[4]{0:T(128)S(1)}, s32[4]{0:T(128)}, u32[]{:S(2)}) copy-start(s32[4]{0:T(128)} %param.15) | copy-start | bytes 52
  10.6 219.2 %all-to-all-start = ((bf16[64,2,512]{2,1,0:T(2,128)(2,1)}), bf16[64,2,512]{2,1,0:T(2,128)(2,1)S(1)}, u32[]{:S(2)}, u32[]{:S(2)}) async-start(bf16[64,2,512]{2,1,0:T(2,128)(2,1)} %reshape.582), calls=%async_computation | async-start | bytes 262144 | tf_op jit(solution)/shard_map/all_to_all | solution.py:8
  29.3 1027.3 %reduce-scatter.2.cloned.1.call-start = ((), (), s32[]{:S(2)}) async-start(), calls=%async_computation.2 | async-start | bytes 2129920 | tf_op jit(solution)/shard_map/reduce_scatter | solution.py:136
  29.4 200.8 %copy-start.4 = (s32[1,512]{1,0:T(1,128)}, s32[1,512]{1,0:T(1,128)S(1)}, u32[]{:S(2)}) copy-start(s32[1,512]{1,0:T(1,128)S(1)} %and_select_fusion.7) | copy-start | bytes 6148
  29.4 1.5 copy-start.8
  29.4 200.8 %copy-start.6 = (s32[1,512]{1,0:T(1,128)}, s32[1,512]{1,0:T(1,128)S(1)}, u32[]{:S(2)}) copy-start(s32[1,512]{1,0:T(1,128)S(1)} %get-tuple-element.285) | copy-start | bytes 6148
  292.9 1.0 copy-start.11
  293.9 69.7 %copy-start.13 = (s32[48]{0:T(128)S(1)}, s32[48]{0:T(128)}, u32[]{:S(2)}) copy-start(s32[48]{0:T(128)} %fusion.108) | copy-start | bytes 580
  293.9 3.2 copy-start.1
  305.8 5.5 copy-start.2
  311.3 3.2 copy-start.1
  323.2 5.5 copy-start.2
  328.7 3.2 copy-start.1
  340.5 5.5 copy-start.2
  346.0 3.2 copy-start.1
  357.9 5.5 copy-start.2
  363.4 3.8 copy-start.10
  363.4 4.0 copy-start.5
  363.4 4.0 copy-start.7
  363.4 4.0 copy-start.9
  363.6 718.0 %copy-start.3 = (bf16[3,1024]{1,0:T(4,128)(2,1)S(1)}, bf16[3,1024]{1,0:T(4,128)(2,1)}, u32[]{:S(2)}) copy-start(bf16[3,1024]{1,0:T(4,128)(2,1)} %param.10) | copy-start | bytes 18436
  365.8 1.3 copy-start
Sparse Core Ops, SparseCore 0:
  367.3 689.2 reduce-scatter.1
